TPU v7x, 32 devices: a whole 2x2x4 slice. The times are simulated.
32 devices in a mesh: seq: 8 (over z, x), head: 4 (over y, core).
Axes of the slice: x: 2, y: 2, z: 4, core: 2. Of those that a mesh axis runs over, the one named last changes fastest.
Arguments:
- queries: bfloat16 [2048, 4096], P('seq', 'head'), may hold values from -100 to 100
- keys_values: bfloat16 [2048, 2, 512], P('seq', None, 'head'), may hold values from -4.5 to 4.5
- cache_kv: bfloat16 [2048, 2, 512], P('seq', None, 'head'), may hold values from -4 to 4
- vertical_pages: int32 [4, 4], P('head'), may hold values from 0 to 15, as said below
- slash_shift: int32 [4, 3], P('head'), may hold values from 1 to 8, as said below
- slash_live: int32 [8, 4, 3], P('seq', 'head'), may hold values 0 or 1
- out_proj: bfloat16 [4096, 2048], P('head'), may hold values from -0.09375 to 0.09375
Outputs:
- projected: bfloat16 [2048, 2048], P('seq', 'head')
Inputs may be any that keep to these rules, and one draw needn't show every extreme that they name: `vertical_pages`: each head group lists 4 distinct pages. `slash_shift`: each head group lists 3 distinct distances.
All inputs are finite; a program needn't handle non-finite values. No bound on the sum of `slash_live` on one device may be relied on, other than what follows from the above.
Results may differ from a plain program's by a relative error of at most 0.0057.
Values may be sent and summed in bfloat16 or wider, within the bound.
No kernel may reach another device: no remote copies, remote signals or barrier semaphores. Data moves between devices by JAX's collectives and lax.ppermute only.
A program may use at most 64 MiB of HBM per device.

v0:
```python
import jax
import jax.numpy as jnp
from jax import lax
from jax.sharding import PartitionSpec as P

PAGE = 128


def passed_along(value, axis, steps):
    count = lax.axis_size(axis)
    pairs = [(source, (source + steps) % count) for source in range(count)]
    return lax.ppermute(value, axis, pairs)


def rotate(stacked, amounts, shards):
    reduced = amounts % shards
    for bit_number in range(max(1, (shards - 1).bit_length())):
        moved = passed_along(stacked, "seq", 1 << bit_number)
        chosen = reduced // (1 << bit_number) % 2 == 1
        stacked = jnp.where(chosen[:, None, None, None], moved, stacked)
    return stacked


def body(queries, keys_values, cache_kv, vertical_pages, slash_shift, slash_live, out_proj):
    row_count = queries.shape[0]
    head_width = keys_values.shape[2]
    group_heads = queries.shape[1] // head_width
    shards = lax.axis_size("seq")
    own_shard = lax.axis_index("seq")
    distances = slash_shift[0]
    live_blocks = slash_live[0, 0] == 1
    page_ids = vertical_pages[0]
    slash_count = distances.shape[0]
    payload = jnp.where(
        (own_shard < shards - distances)[:, None, None, None], keys_values[None], cache_kv[None]
    )
    slash_kv = jnp.concatenate(
        [
            rotate(payload[position : position + 1], distances[position : position + 1], shards)
            for position in range(slash_count)
        ],
        0,
    )
    per_shard = row_count // PAGE
    owners = page_ids // per_shard
    whole_cache = lax.all_gather(cache_kv, "seq", axis=0, tiled=True)
    vertical = jax.vmap(
        lambda page_key: lax.dynamic_slice_in_dim(whole_cache, page_key * PAGE, PAGE, 0)
    )(page_ids)
    cached_slash = own_shard + shards - distances
    clash = (
        live_blocks[None, :]
        & (distances[None, :] > own_shard)
        & (owners[:, None] == cached_slash[None, :])
    )
    page_open = jnp.logical_not(jnp.any(clash, axis=1))
    row_ids = lax.broadcasted_iota(jnp.int32, (row_count, row_count), 0)
    col_ids = lax.broadcasted_iota(jnp.int32, (row_count, row_count), 1)
    causal = row_ids >= col_ids
    column_open = jnp.concatenate([jnp.repeat(live_blocks, row_count), jnp.repeat(page_open, PAGE)])
    visible = jnp.concatenate(
        [causal, jnp.broadcast_to(column_open[None, :], (row_count, column_open.shape[0]))], 1
    )
    all_keys = jnp.concatenate(
        [keys_values, slash_kv.reshape(-1, 2, head_width), vertical.reshape(-1, 2, head_width)], 0
    )
    query_heads = queries.reshape(row_count, group_heads, head_width)
    scores = jnp.einsum(
        "rgd,kd->grk", query_heads, all_keys[:, 0, :], preferred_element_type=jnp.float32
    )
    scores = scores * head_width ** (-0.5)
    scores = jnp.where(visible[None], scores, -jnp.inf)
    row_max = jnp.max(scores, axis=2, keepdims=True)
    weights = jnp.exp(scores - row_max)
    row_total = jnp.sum(weights, axis=2, keepdims=True)
    weights_bf = (weights / row_total).astype(jnp.bfloat16)
    attended = jnp.einsum(
        "grk,kd->rgd", weights_bf, all_keys[:, 1, :], preferred_element_type=jnp.float32
    )
    attended = attended.astype(jnp.bfloat16).reshape(row_count, group_heads * head_width)
    group_terms = jnp.dot(attended, out_proj, preferred_element_type=jnp.float32)
    return lax.psum_scatter(group_terms, "head", scatter_dimension=1, tiled=True).astype(
        jnp.bfloat16
    )


def solution(mesh):
    placed = (
        P("seq", "head"),
        P("seq", None, "head"),
        P("seq", None, "head"),
        P("head", None),
        P("head", None),
        P("seq", "head", None),
        P("head", None),
    )
    return jax.shard_map(
        body, mesh=mesh, in_specs=placed, out_specs=P("seq", "head"), check_vma=False
    )
```

profile of v0, /device:TPU:0, one launch (start us, length us, event | category | flops | bytes accessed | tf_op | source)
XLA Modules:
  0.0 124.2 jit_solution(2235613061482874402)
XLA Ops:
  6.5 0.7 all-gather.2.cloned.1.call-update
  7.3 0.9 copy.23
  8.2 0.9 copy.25
  9.2 0.7 compare_bitcast_fusion
  10.0 3.0 %collective-permute-start = (bf16[1,256,2,128]{3,1,0,2:T(8,128)(2,1)S(1)}, bf16[1,256,2,128]{3,1,0,2:T(8,128)(2,1)S(1)}, u32[]{:S(2)}, u32[]{:S(2)}) collective-permute-start(bf16[1,256,2,128]{3,1,0,2:T(8,128)(2,1)S(1)} %get-tuple-element.8), channel_id=1, source_target_pairs={{0,4},{4,8},{8,12},{12,16},{16,20},{20,24},{24,28},{28,0},{1,5},{5... | collective-permute-start | bytes 393224 | tf_op jit(solution)/shard_map/ppermute | solution.py:12
  13.0 1.5 %collective-permute-start.6 = (bf16[1,256,2,128]{3,1,0,2:T(8,128)(2,1)S(1)}, bf16[1,256,2,128]{3,1,0,2:T(8,128)(2,1)S(1)}, u32[]{:S(2)}, u32[]{:S(2)}) collective-permute-start(bf16[1,256,2,128]{3,1,0,2:T(8,128)(2,1)S(1)} %get-tuple-element.9), channel_id=1, source_target_pairs={{0,4},{4,8},{8,12},{12,16},{16,20},{20,24},{24,28},{28,0},{1,5},{5... | collective-permute-start | bytes 393224 | tf_op jit(solution)/shard_map/ppermute | solution.py:12
  14.6 1.5 %collective-permute-start.3 = (bf16[1,256,2,128]{3,1,0,2:T(8,128)(2,1)S(1)}, bf16[1,256,2,128]{3,1,0,2:T(8,128)(2,1)S(1)}, u32[]{:S(2)}, u32[]{:S(2)}) collective-permute-start(bf16[1,256,2,128]{3,1,0,2:T(8,128)(2,1)S(1)} %get-tuple-element.10), channel_id=1, source_target_pairs={{0,4},{4,8},{8,12},{12,16},{16,20},{20,24},{24,28},{28,0},{1,5},{5... | collective-permute-start | bytes 393224 | tf_op jit(solution)/shard_map/ppermute | solution.py:12
  16.1 0.7 compare_bitcast_fusion.1
  16.7 0.7 subtract_bitcast_fusion
  17.4 0.7 and_select_fusion
  18.5 0.3 pad_add_fusion
  18.7 1.4 %fusion.27 = (s32[1,1]{1,0:T(1,128)}, s32[1,1]{1,0:T(1,128)}, s32[1,1]{1,0:T(1,128)}) fusion(s32[1,3]{1,0:T(1,128)} %param.11), kind=kLoop, calls=%fused_computation.53 | loop fusion | bytes 24 | tf_op jit(solution)/shard_map/slice | solution.py:39
  26.0 1.6 %collective-permute-start.1 = (bf16[1,256,2,128]{3,1,0,2:T(8,128)(2,1)S(1)}, bf16[1,256,2,128]{3,1,0,2:T(8,128)(2,1)S(1)}, u32[]{:S(2)}, u32[]{:S(2)}) collective-permute-start(bf16[1,256,2,128]{3,1,0,2:T(8,128)(2,1)S(1)} %get-tuple-element.5), channel_id=1, source_target_pairs={{0,8},{4,12},{8,16},{12,20},{16,24},{20,28},{24,0},{28,4},{1,9},{5... | collective-permute-start | bytes 393224 | tf_op jit(solution)/shard_map/ppermute | solution.py:12
  27.6 0.7 fusion.23
  28.3 1.6 %collective-permute-start.4 = (bf16[1,256,2,128]{3,1,0,2:T(8,128)(2,1)S(1)}, bf16[1,256,2,128]{3,1,0,2:T(8,128)(2,1)S(1)}, u32[]{:S(2)}, u32[]{:S(2)}) collective-permute-start(bf16[1,256,2,128]{3,1,0,2:T(8,128)(2,1)S(1)} %get-tuple-element.6), channel_id=1, source_target_pairs={{0,8},{4,12},{8,16},{12,20},{16,24},{20,28},{24,0},{28,4},{1,9},{5... | collective-permute-start | bytes 393224 | tf_op jit(solution)/shard_map/ppermute | solution.py:12
  29.9 0.3 collective-permute-start.7
  30.2 4.6 %collective-permute-done.1 = bf16[1,256,2,128]{3,1,0,2:T(8,128)(2,1)S(1)} collective-permute-done((bf16[1,256,2,128]{3,1,0,2:T(8,128)(2,1)S(1)}, bf16[1,256,2,128]{3,1,0,2:T(8,128)(2,1)S(1)}, u32[]{:S(2)}, u32[]{:S(2)}) %collective-permute-start.1) | collective-permute-done | bytes 131104 | tf_op jit(solution)/shard_map/ppermute | solution.py:12
  34.8 1.5 %collective-permute-start.2 = (bf16[1,256,2,128]{3,1,0,2:T(8,128)(2,1)S(1)}, bf16[1,256,2,128]{3,1,0,2:T(8,128)(2,1)S(1)}, u32[]{:S(2)}, u32[]{:S(2)}) collective-permute-start(bf16[1,256,2,128]{3,1,0,2:T(8,128)(2,1)S(1)} %broadcast_select_fusion.8), channel_id=1, source_target_pairs={{0,16},{4,20},{8,24},{12,28},{16,0},{20,4},{24,8},{28,12},{1,17},{... | collective-permute-start | bytes 393224 | tf_op jit(solution)/shard_map/ppermute | solution.py:12
  36.3 1.3 %collective-permute-done.4 = bf16[1,256,2,128]{3,1,0,2:T(8,128)(2,1)S(1)} collective-permute-done((bf16[1,256,2,128]{3,1,0,2:T(8,128)(2,1)S(1)}, bf16[1,256,2,128]{3,1,0,2:T(8,128)(2,1)S(1)}, u32[]{:S(2)}, u32[]{:S(2)}) %collective-permute-start.4) | collective-permute-done | bytes 131104 | tf_op jit(solution)/shard_map/ppermute | solution.py:12
  37.6 1.5 %collective-permute-start.5 = (bf16[1,256,2,128]{3,1,0,2:T(8,128)(2,1)S(1)}, bf16[1,256,2,128]{3,1,0,2:T(8,128)(2,1)S(1)}, u32[]{:S(2)}, u32[]{:S(2)}) collective-permute-start(bf16[1,256,2,128]{3,1,0,2:T(8,128)(2,1)S(1)} %broadcast_select_fusion.5), channel_id=1, source_target_pairs={{0,16},{4,20},{8,24},{12,28},{16,0},{20,4},{24,8},{28,12},{1,17},{... | collective-permute-start | bytes 393224 | tf_op jit(solution)/shard_map/ppermute | solution.py:12
  39.1 1.3 %collective-permute-done.7 = bf16[1,256,2,128]{3,1,0,2:T(8,128)(2,1)S(1)} collective-permute-done((bf16[1,256,2,128]{3,1,0,2:T(8,128)(2,1)S(1)}, bf16[1,256,2,128]{3,1,0,2:T(8,128)(2,1)S(1)}, u32[]{:S(2)}, u32[]{:S(2)}) %collective-permute-start.7) | collective-permute-done | bytes 131104 | tf_op jit(solution)/shard_map/ppermute | solution.py:12
  40.4 8.5 %collective-permute-start.8 = (bf16[1,256,2,128]{3,1,0,2:T(8,128)(2,1)S(1)}, bf16[1,256,2,128]{3,1,0,2:T(8,128)(2,1)S(1)}, u32[]{:S(2)}, u32[]{:S(2)}) collective-permute-start(bf16[1,256,2,128]{3,1,0,2:T(8,128)(2,1)S(1)} %broadcast_select_fusion.2), channel_id=1, source_target_pairs={{0,16},{4,20},{8,24},{12,28},{16,0},{20,4},{24,8},{28,12},{1,17},{... | collective-permute-start | bytes 393224 | tf_op jit(solution)/shard_map/ppermute | solution.py:12
  49.0 0.7 collective-permute-done.2
  49.7 4.2 %collective-permute-done.5 = bf16[1,256,2,128]{3,1,0,2:T(8,128)(2,1)S(1)} collective-permute-done((bf16[1,256,2,128]{3,1,0,2:T(8,128)(2,1)S(1)}, bf16[1,256,2,128]{3,1,0,2:T(8,128)(2,1)S(1)}, u32[]{:S(2)}, u32[]{:S(2)}) %collective-permute-start.5) | collective-permute-done | bytes 131104 | tf_op jit(solution)/shard_map/ppermute | solution.py:12
  53.9 6.4 %collective-permute-done.8 = bf16[1,256,2,128]{3,1,0,2:T(8,128)(2,1)S(1)} collective-permute-done((bf16[1,256,2,128]{3,1,0,2:T(8,128)(2,1)S(1)}, bf16[1,256,2,128]{3,1,0,2:T(8,128)(2,1)S(1)}, u32[]{:S(2)}, u32[]{:S(2)}) %collective-permute-start.8) | collective-permute-done | bytes 131104 | tf_op jit(solution)/shard_map/ppermute | solution.py:12
  60.4 7.5 %all-gather.2.cloned.1.call-done = bf16[2048,2,128]{2,1,0:T(2,128)(2,1)} async-done(((bf16[256,2,128]{2,1,0:T(2,128)(2,1)}), bf16[2048,2,128]{2,1,0:T(2,128)(2,1)}) %all-gather.2.cloned.1.call-update) | async-done | bytes 1048592 | tf_op jit(solution)/shard_map/all_gather | solution.py:46
  67.8 2.3 %gather_fusion = bf16[4,128,2,128]{3,2,1,0:T(2,128)(2,1)S(1)} fusion(bf16[2048,2,128]{2,1,0:T(2,128)(2,1)} %all-gather.2.cloned.1.call-done, s32[4]{0:T(128)S(1)} %fusion.23), kind=kCustom, calls=%fused_computation | custom fusion | bytes 524336 | tf_op jit(solution)/shard_map/vmap()/gather | solution.py:48
  70.3 6.9 %fusion.28 = (f32[8,256]{1,0:T(8,128)S(1)}, f32[8,256,1536]{1,2,0:T(8,128)}) fusion(pred[256,1536]{0,1:T(8,128)(4,1)S(1)} %pad_add_fusion, bf16[1536,2,128]{2,0,1:T(8,128)(2,1)S(1)} %pad_maximum_fusion, bf16[256,1024]{1,0:T(8,128)(2,1)S(1)} %copy-done), kind=kOutput, calls=%fused_computation.54 | convolution fusion | flops 817890816 | bytes 13901824 | tf_op jit(solution)/shard_map/sub | solution.py:74
  77.2 5.7 %fusion.8 = bf16[128,8,256]{2,0,1:T(8,128)(2,1)S(1)} fusion(f32[8,256,1536]{1,2,0:T(8,128)} %get-tuple-element.17, f32[8,256]{1,0:T(8,128)S(1)} %get-tuple-element.16, bf16[1536,2,128]{2,0,1:T(8,128)(2,1)S(1)} %pad_maximum_fusion), kind=kOutput, calls=%fused_computation.12 | convolution fusion | flops 811859968 | bytes 13508608 | tf_op jit(solution)/shard_map/grk,kd->rgd/dot_general | solution.py:77
  83.0 2.6 %fusion.33 = f32[256,2048]{1,0:T(8,128)} fusion(bf16[256,1024]{0,1:T(8,128)(2,1)S(1)} %bitcast.95, bf16[1024,2048]{1,0:T(8,128)(2,1)S(1)} %copy-done.1), kind=kOutput, calls=%fused_computation.55 | convolution fusion | flops 1073741824 | bytes 6815744 | tf_op jit(solution)/shard_map/dot_general | solution.py:81
  85.6 30.0 %reduce-scatter.2.cloned.1.call-done = f32[256,512]{1,0:T(8,128)} async-done(((f32[256,2048]{1,0:T(8,128)}), f32[256,512]{1,0:T(8,128)}) %reduce-scatter.2.cloned.1.call-update) | async-done | bytes 524304 | tf_op jit(solution)/shard_map/reduce_scatter | solution.py:82
  115.6 1.8 %convert_element_type.15 = bf16[256,512]{1,0:T(8,128)(2,1)} convert(f32[256,512]{1,0:T(8,128)} %reduce-scatter.2.cloned.1.call-done) | non-fusion elementwise | flops 131072 | bytes 786432 | tf_op jit(solution)/shard_map/convert_element_type | solution.py:82
  (30 shorter events, 0.9 us)
Async XLA Ops:
  6.5 63.7 %copy-start = (bf16[256,1024]{1,0:T(8,128)(2,1)S(1)}, bf16[256,1024]{1,0:T(8,128)(2,1)}, u32[]{:S(2)}) copy-start(bf16[256,1024]{1,0:T(8,128)(2,1)} %param.7) | copy-start | bytes 1572868
  6.5 61.3 %all-gather.2.cloned.1.call-start = ((), (), s32[]{:S(2)}) async-start(), calls=%async_computation.1 | async-start | bytes 1179648 | tf_op jit(solution)/shard_map/all_gather | solution.py:46
  7.3 108.3 %reduce-scatter.2.cloned.1.call-start = ((), (), s32[]{:S(2)}) async-start(), calls=%async_computation.2 | async-start | bytes 2621440 | tf_op jit(solution)/shard_map/reduce_scatter | solution.py:82
  10.0 15.9 %collective-permute-start = (bf16[1,256,2,128]{3,1,0,2:T(8,128)(2,1)S(1)}, bf16[1,256,2,128]{3,1,0,2:T(8,128)(2,1)S(1)}, u32[]{:S(2)}, u32[]{:S(2)}) collective-permute-start(bf16[1,256,2,128]{3,1,0,2:T(8,128)(2,1)S(1)} %get-tuple-element.8), channel_id=1, source_target_pairs={{0,4},{4,8},{8,12},{12,16},{16,20},{20,24},{24,28},{28,0},{1,5},{5... | collective-permute-start | bytes 393224 | tf_op jit(solution)/shard_map/ppermute | solution.py:12
  13.0 12.9 %collective-permute-start.6 = (bf16[1,256,2,128]{3,1,0,2:T(8,128)(2,1)S(1)}, bf16[1,256,2,128]{3,1,0,2:T(8,128)(2,1)S(1)}, u32[]{:S(2)}, u32[]{:S(2)}) collective-permute-start(bf16[1,256,2,128]{3,1,0,2:T(8,128)(2,1)S(1)} %get-tuple-element.9), channel_id=1, source_target_pairs={{0,4},{4,8},{8,12},{12,16},{16,20},{20,24},{24,28},{28,0},{1,5},{5... | collective-permute-start | bytes 393224 | tf_op jit(solution)/shard_map/ppermute | solution.py:12
  14.6 11.4 %collective-permute-start.3 = (bf16[1,256,2,128]{3,1,0,2:T(8,128)(2,1)S(1)}, bf16[1,256,2,128]{3,1,0,2:T(8,128)(2,1)S(1)}, u32[]{:S(2)}, u32[]{:S(2)}) collective-permute-start(bf16[1,256,2,128]{3,1,0,2:T(8,128)(2,1)S(1)} %get-tuple-element.10), channel_id=1, source_target_pairs={{0,4},{4,8},{8,12},{12,16},{16,20},{20,24},{24,28},{28,0},{1,5},{5... | collective-permute-start | bytes 393224 | tf_op jit(solution)/shard_map/ppermute | solution.py:12
  26.0 8.8 %collective-permute-start.1 = (bf16[1,256,2,128]{3,1,0,2:T(8,128)(2,1)S(1)}, bf16[1,256,2,128]{3,1,0,2:T(8,128)(2,1)S(1)}, u32[]{:S(2)}, u32[]{:S(2)}) collective-permute-start(bf16[1,256,2,128]{3,1,0,2:T(8,128)(2,1)S(1)} %get-tuple-element.5), channel_id=1, source_target_pairs={{0,8},{4,12},{8,16},{12,20},{16,24},{20,28},{24,0},{28,4},{1,9},{5... | collective-permute-start | bytes 393224 | tf_op jit(solution)/shard_map/ppermute | solution.py:12
  28.3 9.3 %collective-permute-start.4 = (bf16[1,256,2,128]{3,1,0,2:T(8,128)(2,1)S(1)}, bf16[1,256,2,128]{3,1,0,2:T(8,128)(2,1)S(1)}, u32[]{:S(2)}, u32[]{:S(2)}) collective-permute-start(bf16[1,256,2,128]{3,1,0,2:T(8,128)(2,1)S(1)} %get-tuple-element.6), channel_id=1, source_target_pairs={{0,8},{4,12},{8,16},{12,20},{16,24},{20,28},{24,0},{28,4},{1,9},{5... | collective-permute-start | bytes 393224 | tf_op jit(solution)/shard_map/ppermute | solution.py:12
  29.9 10.5 %collective-permute-start.7 = (bf16[1,256,2,128]{3,1,0,2:T(8,128)(2,1)S(1)}, bf16[1,256,2,128]{3,1,0,2:T(8,128)(2,1)S(1)}, u32[]{:S(2)}, u32[]{:S(2)}) collective-permute-start(bf16[1,256,2,128]{3,1,0,2:T(8,128)(2,1)S(1)} %get-tuple-element.7), channel_id=1, source_target_pairs={{0,8},{4,12},{8,16},{12,20},{16,24},{20,28},{24,0},{28,4},{1,9},{5... | collective-permute-start | bytes 393224 | tf_op jit(solution)/shard_map/ppermute | solution.py:12
  34.8 14.8 %collective-permute-start.2 = (bf16[1,256,2,128]{3,1,0,2:T(8,128)(2,1)S(1)}, bf16[1,256,2,128]{3,1,0,2:T(8,128)(2,1)S(1)}, u32[]{:S(2)}, u32[]{:S(2)}) collective-permute-start(bf16[1,256,2,128]{3,1,0,2:T(8,128)(2,1)S(1)} %broadcast_select_fusion.8), channel_id=1, source_target_pairs={{0,16},{4,20},{8,24},{12,28},{16,0},{20,4},{24,8},{28,12},{1,17},{... | collective-permute-start | bytes 393224 | tf_op jit(solution)/shard_map/ppermute | solution.py:12
  37.6 16.2 %collective-permute-start.5 = (bf16[1,256,2,128]{3,1,0,2:T(8,128)(2,1)S(1)}, bf16[1,256,2,128]{3,1,0,2:T(8,128)(2,1)S(1)}, u32[]{:S(2)}, u32[]{:S(2)}) collective-permute-start(bf16[1,256,2,128]{3,1,0,2:T(8,128)(2,1)S(1)} %broadcast_select_fusion.5), channel_id=1, source_target_pairs={{0,16},{4,20},{8,24},{12,28},{16,0},{20,4},{24,8},{28,12},{1,17},{... | collective-permute-start | bytes 393224 | tf_op jit(solution)/shard_map/ppermute | solution.py:12
  40.4 19.8 %collective-permute-start.8 = (bf16[1,256,2,128]{3,1,0,2:T(8,128)(2,1)S(1)}, bf16[1,256,2,128]{3,1,0,2:T(8,128)(2,1)S(1)}, u32[]{:S(2)}, u32[]{:S(2)}) collective-permute-start(bf16[1,256,2,128]{3,1,0,2:T(8,128)(2,1)S(1)} %broadcast_select_fusion.2), channel_id=1, source_target_pairs={{0,16},{4,20},{8,24},{12,28},{16,0},{20,4},{24,8},{28,12},{1,17},{... | collective-permute-start | bytes 393224 | tf_op jit(solution)/shard_map/ppermute | solution.py:12
  77.2 5.8 %copy-start.1 = (bf16[1024,2048]{1,0:T(8,128)(2,1)S(1)}, bf16[1024,2048]{1,0:T(8,128)(2,1)}, u32[]{:S(2)}) copy-start(bf16[1024,2048]{1,0:T(8,128)(2,1)} %param.13) | copy-start | bytes 12582916
Sparse Core Ops, SparseCore 0:
  9.5 58.3 all-gather.1
  85.7 29.8 reduce-scatter.1
where the time goes:
time: 125 us; the launch traced here: 124 us
  waiting for transfers between devices  56.7 us (45%)
  starting transfers between devices  21.1 us (17%)
  between operations  19.4 us (16%)
  matrix products  15.3 us (12%)
  other arithmetic  5.95 us (5%)
  local copies, waits for them, and re-layouts  5.8 us (5%)
    reduce_scatter x1, waiting for transfers between devices, body(): lax.psum_scatter(group_terms, 'head', scatter_dimension=1, tiled=True)  30 us
    ppermute x9, starting transfers between devices, passed_along(): return lax.ppermute(value, axis, pairs)  21.1 us
    ppermute x9, waiting for transfers between devices, passed_along(): return lax.ppermute(value, axis, pairs)  18.5 us
    all_gather x1, waiting for transfers between devices, body(): whole_cache = lax.all_gather(cache_kv, 'seq', axis=0, tiled=True)  7.47 us
    sub x1, matrix products, body(): weights = jnp.exp(scores - row_max)  6.94 us
    dot_general x1, matrix products, body(): jnp.einsum('grk,kd->rgd', weights_bf, all_keys[:, 1, :], preferred_elemen...  5.73 us
    dot_general x1, matrix products, body(): jnp.dot(attended, out_proj, preferred_element_type=jnp.float32)  2.61 us
  transfers between devices with their start and end apart: 11, of which 8 were waited for; matrix products, arithmetic and copies ran while one was open for 6% of the time, Pallas kernels for 0%

commit v1 on v0

--- a/solution.py
+++ b/solution.py
@@ -4,6 +4,23 @@
 from jax.sharding import PartitionSpec as P
 
 PAGE = 128
+
+
+def divide_members_all(m):
+    upper, carry_in, block_next = (lax.psum(1, "seq"), lax.axis_index("seq"), m.shape[0])
+    shaped, oldest = (m, 1)
+    while oldest < upper:
+        shaped = jnp.concatenate(
+            [
+                shaped,
+                lax.ppermute(
+                    shaped, "seq", tuple(((kk, (kk - oldest) % upper) for kk in range(upper)))
+                ),
+            ],
+            0,
+        )
+        oldest = 2 * oldest
+    return jnp.roll(shaped, carry_in * block_next, 0)
 
 
 def passed_along(value, axis, steps):
@@ -43,7 +60,7 @@
     )
     per_shard = row_count // PAGE
     owners = page_ids // per_shard
-    whole_cache = lax.all_gather(cache_kv, "seq", axis=0, tiled=True)
+    whole_cache = divide_members_all(cache_kv)
     vertical = jax.vmap(
         lambda page_key: lax.dynamic_slice_in_dim(whole_cache, page_key * PAGE, PAGE, 0)
     )(page_ids)

time: 125 us -> 143 us (1.14)
  waiting for transfers between devices: 56.7 us -> 78.9 us
  starting transfers between devices: 21.1 us -> 16.1 us
    ppermute x9, waiting for transfers between devices: 18.5 us -> 37.2 us  [passed_along(): return lax.ppermute(value, axis, pairs)]
    ppermute x9, starting transfers between devices: 21.1 us -> 3.66 us  [passed_along(): return lax.ppermute(value, axis, pairs)]
    ppermute x0 -> x3, starting transfers between devices: none -> 12.4 us  [divide_members_all(): lax.ppermute(shaped, 'seq', tuple(((kk, (kk - oldest) % upper) for kk in...]
    ppermute x0 -> x3, waiting for transfers between devices: none -> 10.5 us  [divide_members_all(): lax.ppermute(shaped, 'seq', tuple(((kk, (kk - oldest) % upper) for kk in...]
    all_gather x1 -> x0, waiting for transfers between devices: 7.47 us -> none  [body(): whole_cache = lax.all_gather(cache_kv, 'seq', axis=0, tiled=True)]
    unnamed x6 -> x17, local copies, waits for them, and re-layouts: 1.88 us -> 3.18 us
  transfers between devices with their start and end apart: 11 -> 13, of which waited for: 8 -> 10; matrix products, arithmetic and copies ran while one was open for 6% -> 6% of each run, Pallas kernels for 0% -> 0%
where the time goes in v1:
time: 143 us
  waiting for transfers between devices  78.9 us (55%)
  between operations  19.4 us (14%)
  starting transfers between devices  16.1 us (11%)
  matrix products  15.3 us (11%)
  other arithmetic  7.02 us (5%)
  local copies, waits for them, and re-layouts  6.3 us (4%)
    ppermute x9, waiting for transfers between devices, passed_along(): return lax.ppermute(value, axis, pairs)  37.2 us
    reduce_scatter x1, waiting for transfers between devices, body(): lax.psum_scatter(group_terms, 'head', scatter_dimension=1, tiled=True)  31.1 us
    ppermute x3, starting transfers between devices, divide_members_all(): lax.ppermute(shaped, 'seq', tuple(((kk, (kk - oldest) % upper) for kk in...  12.4 us
    ppermute x3, waiting for transfers between devices, divide_members_all(): lax.ppermute(shaped, 'seq', tuple(((kk, (kk - oldest) % upper) for kk in...  10.5 us
    sub x1, matrix products, body(): weights = jnp.exp(scores - row_max)  6.99 us
    dot_general x1, matrix products, body(): jnp.einsum('grk,kd->rgd', weights_bf, all_keys[:, 1, :], preferred_elemen...  5.75 us
    ppermute x9, starting transfers between devices, passed_along(): return lax.ppermute(value, axis, pairs)  3.66 us
    unnamed x17, local copies, waits for them, and re-layouts  3.18 us
  transfers between devices with their start and end apart: 13, of which 10 were waited for; matrix products, arithmetic and copies ran while one was open for 6% of the time, Pallas kernels for 0%

profile of v1, /device:TPU:0, one launch (start us, length us, event | category | flops | bytes accessed | tf_op | source)
XLA Modules:
  0.0 143.0 jit_solution(8583588583465561222)
XLA Ops:
  6.5 6.1 %collective-permute-start.9 = (bf16[256,2,128]{2,1,0:T(2,128)(2,1)}, bf16[256,2,128]{2,1,0:T(2,128)(2,1)S(1)}, u32[]{:S(2)}, u32[]{:S(2)}) collective-permute-start(bf16[256,2,128]{2,1,0:T(2,128)(2,1)} %param.9), channel_id=1, source_target_pairs={{0,28},{4,0},{8,4},{12,8},{16,12},{20,16},{24,20},{28,24},{1,29},{... | collective-permute-start | bytes 393224 | tf_op jit(solution)/shard_map/ppermute | solution.py:16
  12.6 1.0 copy.16
  13.6 0.9 copy.18
  14.5 0.7 compare_bitcast_fusion
  15.5 0.5 collective-permute-start.3
  15.9 0.7 and_select_fusion
  16.6 0.7 fusion.23
  17.2 0.7 compare_bitcast_fusion.1
  17.9 0.7 subtract_bitcast_fusion
  19.3 0.6 fusion.27
  25.8 1.4 collective-permute-done.6
  27.2 1.4 collective-permute-done.3
  29.1 3.9 %collective-permute-start.10 = (bf16[512,2,128]{2,1,0:T(2,128)(2,1)S(1)}, bf16[512,2,128]{2,1,0:T(2,128)(2,1)S(1)}, u32[]{:S(2)}, u32[]{:S(2)}) collective-permute-start(bf16[512,2,128]{2,1,0:T(2,128)(2,1)S(1)} %pad_maximum_fusion.3), channel_id=1, source_target_pairs={{0,24},{4,28},{8,0},{12,4},{16,8},{20,12},{24,16},{28,20},{1,25},{... | collective-permute-start | bytes 786440 | tf_op jit(solution)/shard_map/ppermute | solution.py:16
  33.1 3.8 %collective-permute-done.1 = bf16[1,256,2,128]{3,1,0,2:T(8,128)(2,1)S(1)} collective-permute-done((bf16[1,256,2,128]{3,1,0,2:T(8,128)(2,1)S(1)}, bf16[1,256,2,128]{3,1,0,2:T(8,128)(2,1)S(1)}, u32[]{:S(2)}, u32[]{:S(2)}) %collective-permute-start.1) | collective-permute-done | bytes 131104 | tf_op jit(solution)/shard_map/ppermute | solution.py:29
  36.9 2.4 %collective-permute-start.2 = (bf16[1,256,2,128]{3,1,0,2:T(8,128)(2,1)S(1)}, bf16[1,256,2,128]{3,1,0,2:T(8,128)(2,1)S(1)}, u32[]{:S(2)}, u32[]{:S(2)}) collective-permute-start(bf16[1,256,2,128]{3,1,0,2:T(8,128)(2,1)S(1)} %broadcast_select_fusion.8), channel_id=1, source_target_pairs={{0,16},{4,20},{8,24},{12,28},{16,0},{20,4},{24,8},{28,12},{1,17},{... | collective-permute-start | bytes 393224 | tf_op jit(solution)/shard_map/ppermute | solution.py:29
  39.3 6.1 %collective-permute-done.4 = bf16[1,256,2,128]{3,1,0,2:T(8,128)(2,1)S(1)} collective-permute-done((bf16[1,256,2,128]{3,1,0,2:T(8,128)(2,1)S(1)}, bf16[1,256,2,128]{3,1,0,2:T(8,128)(2,1)S(1)}, u32[]{:S(2)}, u32[]{:S(2)}) %collective-permute-start.4) | collective-permute-done | bytes 131104 | tf_op jit(solution)/shard_map/ppermute | solution.py:29
  45.5 2.7 %collective-permute-done.7 = bf16[1,256,2,128]{3,1,0,2:T(8,128)(2,1)S(1)} collective-permute-done((bf16[1,256,2,128]{3,1,0,2:T(8,128)(2,1)S(1)}, bf16[1,256,2,128]{3,1,0,2:T(8,128)(2,1)S(1)}, u32[]{:S(2)}, u32[]{:S(2)}) %collective-permute-start.7) | collective-permute-done | bytes 131104 | tf_op jit(solution)/shard_map/ppermute | solution.py:29
  48.3 0.5 collective-permute-start.8
  48.8 0.7 pad_maximum_fusion.1
  49.5 2.5 %collective-permute-start.11 = (bf16[1024,2,128]{2,1,0:T(2,128)(2,1)S(1)}, bf16[1024,2,128]{2,1,0:T(2,128)(2,1)S(1)}, u32[]{:S(2)}, u32[]{:S(2)}) collective-permute-start(bf16[1024,2,128]{2,1,0:T(2,128)(2,1)S(1)} %pad_maximum_fusion.1), channel_id=1, source_target_pairs={{0,16},{4,20},{8,24},{12,28},{16,0},{20,4},{24,8},{28,12},{1,17},{... | collective-permute-start | bytes 1572872 | tf_op jit(solution)/shard_map/ppermute | solution.py:16
  52.0 16.4 %collective-permute-done.2 = bf16[1,256,2,128]{3,1,0,2:T(8,128)(2,1)S(1)} collective-permute-done((bf16[1,256,2,128]{3,1,0,2:T(8,128)(2,1)S(1)}, bf16[1,256,2,128]{3,1,0,2:T(8,128)(2,1)S(1)}, u32[]{:S(2)}, u32[]{:S(2)}) %collective-permute-start.2) | collective-permute-done | bytes 131104 | tf_op jit(solution)/shard_map/ppermute | solution.py:29
  68.5 2.8 %collective-permute-done.5 = bf16[1,256,2,128]{3,1,0,2:T(8,128)(2,1)S(1)} collective-permute-done((bf16[1,256,2,128]{3,1,0,2:T(8,128)(2,1)S(1)}, bf16[1,256,2,128]{3,1,0,2:T(8,128)(2,1)S(1)}, u32[]{:S(2)}, u32[]{:S(2)}) %collective-permute-start.5) | collective-permute-done | bytes 131104 | tf_op jit(solution)/shard_map/ppermute | solution.py:29
  71.5 2.6 %collective-permute-done.8 = bf16[1,256,2,128]{3,1,0,2:T(8,128)(2,1)S(1)} collective-permute-done((bf16[1,256,2,128]{3,1,0,2:T(8,128)(2,1)S(1)}, bf16[1,256,2,128]{3,1,0,2:T(8,128)(2,1)S(1)}, u32[]{:S(2)}, u32[]{:S(2)}) %collective-permute-start.8) | collective-permute-done | bytes 131104 | tf_op jit(solution)/shard_map/ppermute | solution.py:29
  74.1 10.5 %collective-permute-done.11 = bf16[1024,2,128]{2,1,0:T(2,128)(2,1)S(1)} collective-permute-done((bf16[1024,2,128]{2,1,0:T(2,128)(2,1)S(1)}, bf16[1024,2,128]{2,1,0:T(2,128)(2,1)S(1)}, u32[]{:S(2)}, u32[]{:S(2)}) %collective-permute-start.11) | collective-permute-done | bytes 524320 | tf_op jit(solution)/shard_map/ppermute | solution.py:16
  84.7 0.4 constant_dynamic-update-slice_fusion.4
  85.9 0.8 constant_dynamic-slice_fusion
  86.7 1.1 gather_fusion
  87.9 7.0 %fusion.28 = (f32[8,256]{1,0:T(8,128)S(1)}, f32[8,256,1536]{1,2,0:T(8,128)}) fusion(pred[256,1536]{0,1:T(8,128)(4,1)S(1)} %pad_add_fusion, bf16[1536,2,128]{2,0,1:T(8,128)(2,1)S(1)} %pad_maximum_fusion, bf16[256,1024]{1,0:T(8,128)(2,1)S(1)} %copy-done), kind=kOutput, calls=%fused_computation.65 | convolution fusion | flops 817890816 | bytes 13901824 | tf_op jit(solution)/shard_map/sub | solution.py:91
  94.9 5.7 %fusion.8 = bf16[128,8,256]{2,0,1:T(8,128)(2,1)S(1)} fusion(f32[8,256,1536]{1,2,0:T(8,128)} %get-tuple-element.17, f32[8,256]{1,0:T(8,128)S(1)} %get-tuple-element.16, bf16[1536,2,128]{2,0,1:T(8,128)(2,1)S(1)} %pad_maximum_fusion), kind=kOutput, calls=%fused_computation.12 | convolution fusion | flops 811859968 | bytes 13508608 | tf_op jit(solution)/shard_map/grk,kd->rgd/dot_general | solution.py:94
  100.7 2.6 %fusion.33 = f32[256,2048]{1,0:T(8,128)} fusion(bf16[256,1024]{0,1:T(8,128)(2,1)S(1)} %bitcast.95, bf16[1024,2048]{1,0:T(8,128)(2,1)S(1)} %copy-done.3), kind=kOutput, calls=%fused_computation.66 | convolution fusion | flops 1073741824 | bytes 6815744 | tf_op jit(solution)/shard_map/dot_general | solution.py:98
  103.3 31.1 %reduce-scatter.2.cloned.1.call-done = f32[256,512]{1,0:T(8,128)} async-done(((f32[256,2048]{1,0:T(8,128)}), f32[256,512]{1,0:T(8,128)}) %reduce-scatter.2.cloned.1.call-update) | async-done | bytes 524304 | tf_op jit(solution)/shard_map/reduce_scatter | solution.py:99
  134.4 1.8 %convert_element_type.15 = bf16[256,512]{1,0:T(8,128)(2,1)} convert(f32[256,512]{1,0:T(8,128)} %reduce-scatter.2.cloned.1.call-done) | non-fusion elementwise | flops 131072 | bytes 786432 | tf_op jit(solution)/shard_map/convert_element_type | solution.py:99
  (48 shorter events, 3.0 us)
Async XLA Ops:
  6.5 81.4 %copy-start = (bf16[256,1024]{1,0:T(8,128)(2,1)S(1)}, bf16[256,1024]{1,0:T(8,128)(2,1)}, u32[]{:S(2)}) copy-start(bf16[256,1024]{1,0:T(8,128)(2,1)} %param.7) | copy-start | bytes 1572868
  6.5 19.2 %copy-start.1 = (bf16[256,2,128]{2,1,0:T(2,128)(2,1)S(1)}, bf16[256,2,128]{2,1,0:T(2,128)(2,1)}, u32[]{:S(2)}) copy-start(bf16[256,2,128]{2,1,0:T(2,128)(2,1)} %param.9) | copy-start | bytes 393220
  6.5 12.7 %copy-start.2 = (s32[1,3]{1,0:T(1,128)S(1)}, s32[1,3]{1,0:T(1,128)}, u32[]{:S(2)}) copy-start(s32[1,3]{1,0:T(1,128)} %param.11) | copy-start | bytes 40
  6.5 127.9 %reduce-scatter.2.cloned.1.call-start = ((), (), s32[]{:S(2)}) async-start(), calls=%async_computation.1 | async-start | bytes 2621440 | tf_op jit(solution)/shard_map/reduce_scatter | solution.py:99
  6.5 22.2 %collective-permute-start.9 = (bf16[256,2,128]{2,1,0:T(2,128)(2,1)}, bf16[256,2,128]{2,1,0:T(2,128)(2,1)S(1)}, u32[]{:S(2)}, u32[]{:S(2)}) collective-permute-start(bf16[256,2,128]{2,1,0:T(2,128)(2,1)} %param.9), channel_id=1, source_target_pairs={{0,28},{4,0},{8,4},{12,8},{16,12},{20,16},{24,20},{28,24},{1,29},{... | collective-permute-start | bytes 393224 | tf_op jit(solution)/shard_map/ppermute | solution.py:16
  15.3 10.5 %collective-permute-start = (bf16[1,256,2,128]{3,1,0,2:T(8,128)(2,1)S(1)}, bf16[1,256,2,128]{3,1,0,2:T(8,128)(2,1)S(1)}, u32[]{:S(2)}, u32[]{:S(2)}) collective-permute-start(bf16[1,256,2,128]{3,1,0,2:T(8,128)(2,1)S(1)} %get-tuple-element.8), channel_id=1, source_target_pairs={{0,4},{4,8},{8,12},{12,16},{16,20},{20,24},{24,28},{28,0},{1,5},{5... | collective-permute-start | bytes 393224 | tf_op jit(solution)/shard_map/ppermute | solution.py:29
  15.4 11.9 %collective-permute-start.6 = (bf16[1,256,2,128]{3,1,0,2:T(8,128)(2,1)S(1)}, bf16[1,256,2,128]{3,1,0,2:T(8,128)(2,1)S(1)}, u32[]{:S(2)}, u32[]{:S(2)}) collective-permute-start(bf16[1,256,2,128]{3,1,0,2:T(8,128)(2,1)S(1)} %get-tuple-element.9), channel_id=1, source_target_pairs={{0,4},{4,8},{8,12},{12,16},{16,20},{20,24},{24,28},{28,0},{1,5},{5... | collective-permute-start | bytes 393224 | tf_op jit(solution)/shard_map/ppermute | solution.py:29
  15.5 13.2 %collective-permute-start.3 = (bf16[1,256,2,128]{3,1,0,2:T(8,128)(2,1)S(1)}, bf16[1,256,2,128]{3,1,0,2:T(8,128)(2,1)S(1)}, u32[]{:S(2)}, u32[]{:S(2)}) collective-permute-start(bf16[1,256,2,128]{3,1,0,2:T(8,128)(2,1)S(1)} %get-tuple-element.10), channel_id=1, source_target_pairs={{0,4},{4,8},{8,12},{12,16},{16,20},{20,24},{24,28},{28,0},{1,5},{5... | collective-permute-start | bytes 393224 | tf_op jit(solution)/shard_map/ppermute | solution.py:29
  28.7 8.2 %collective-permute-start.1 = (bf16[1,256,2,128]{3,1,0,2:T(8,128)(2,1)S(1)}, bf16[1,256,2,128]{3,1,0,2:T(8,128)(2,1)S(1)}, u32[]{:S(2)}, u32[]{:S(2)}) collective-permute-start(bf16[1,256,2,128]{3,1,0,2:T(8,128)(2,1)S(1)} %get-tuple-element.5), channel_id=1, source_target_pairs={{0,8},{4,12},{8,16},{12,20},{16,24},{20,28},{24,0},{28,4},{1,9},{5... | collective-permute-start | bytes 393224 | tf_op jit(solution)/shard_map/ppermute | solution.py:29
  29.1 19.7 %collective-permute-start.10 = (bf16[512,2,128]{2,1,0:T(2,128)(2,1)S(1)}, bf16[512,2,128]{2,1,0:T(2,128)(2,1)S(1)}, u32[]{:S(2)}, u32[]{:S(2)}) collective-permute-start(bf16[512,2,128]{2,1,0:T(2,128)(2,1)S(1)} %pad_maximum_fusion.3), channel_id=1, source_target_pairs={{0,24},{4,28},{8,0},{12,4},{16,8},{20,12},{24,16},{28,20},{1,25},{... | collective-permute-start | bytes 786440 | tf_op jit(solution)/shard_map/ppermute | solution.py:16
  33.0 12.5 %collective-permute-start.4 = (bf16[1,256,2,128]{3,1,0,2:T(8,128)(2,1)S(1)}, bf16[1,256,2,128]{3,1,0,2:T(8,128)(2,1)S(1)}, u32[]{:S(2)}, u32[]{:S(2)}) collective-permute-start(bf16[1,256,2,128]{3,1,0,2:T(8,128)(2,1)S(1)} %get-tuple-element.6), channel_id=1, source_target_pairs={{0,8},{4,12},{8,16},{12,20},{16,24},{20,28},{24,0},{28,4},{1,9},{5... | collective-permute-start | bytes 393224 | tf_op jit(solution)/shard_map/ppermute | solution.py:29
  33.0 15.3 %collective-permute-start.7 = (bf16[1,256,2,128]{3,1,0,2:T(8,128)(2,1)S(1)}, bf16[1,256,2,128]{3,1,0,2:T(8,128)(2,1)S(1)}, u32[]{:S(2)}, u32[]{:S(2)}) collective-permute-start(bf16[1,256,2,128]{3,1,0,2:T(8,128)(2,1)S(1)} %get-tuple-element.7), channel_id=1, source_target_pairs={{0,8},{4,12},{8,16},{12,20},{16,24},{20,28},{24,0},{28,4},{1,9},{5... | collective-permute-start | bytes 393224 | tf_op jit(solution)/shard_map/ppermute | solution.py:29
  36.9 31.5 %collective-permute-start.2 = (bf16[1,256,2,128]{3,1,0,2:T(8,128)(2,1)S(1)}, bf16[1,256,2,128]{3,1,0,2:T(8,128)(2,1)S(1)}, u32[]{:S(2)}, u32[]{:S(2)}) collective-permute-start(bf16[1,256,2,128]{3,1,0,2:T(8,128)(2,1)S(1)} %broadcast_select_fusion.8), channel_id=1, source_target_pairs={{0,16},{4,20},{8,24},{12,28},{16,0},{20,4},{24,8},{28,12},{1,17},{... | collective-permute-start | bytes 393224 | tf_op jit(solution)/shard_map/ppermute | solution.py:29
  45.5 25.8 %collective-permute-start.5 = (bf16[1,256,2,128]{3,1,0,2:T(8,128)(2,1)S(1)}, bf16[1,256,2,128]{3,1,0,2:T(8,128)(2,1)S(1)}, u32[]{:S(2)}, u32[]{:S(2)}) collective-permute-start(bf16[1,256,2,128]{3,1,0,2:T(8,128)(2,1)S(1)} %broadcast_select_fusion.5), channel_id=1, source_target_pairs={{0,16},{4,20},{8,24},{12,28},{16,0},{20,4},{24,8},{28,12},{1,17},{... | collective-permute-start | bytes 393224 | tf_op jit(solution)/shard_map/ppermute | solution.py:29
  48.3 25.8 %collective-permute-start.8 = (bf16[1,256,2,128]{3,1,0,2:T(8,128)(2,1)S(1)}, bf16[1,256,2,128]{3,1,0,2:T(8,128)(2,1)S(1)}, u32[]{:S(2)}, u32[]{:S(2)}) collective-permute-start(bf16[1,256,2,128]{3,1,0,2:T(8,128)(2,1)S(1)} %broadcast_select_fusion.2), channel_id=1, source_target_pairs={{0,16},{4,20},{8,24},{12,28},{16,0},{20,4},{24,8},{28,12},{1,17},{... | collective-permute-start | bytes 393224 | tf_op jit(solution)/shard_map/ppermute | solution.py:29
  49.5 35.1 %collective-permute-start.11 = (bf16[1024,2,128]{2,1,0:T(2,128)(2,1)S(1)}, bf16[1024,2,128]{2,1,0:T(2,128)(2,1)S(1)}, u32[]{:S(2)}, u32[]{:S(2)}) collective-permute-start(bf16[1024,2,128]{2,1,0:T(2,128)(2,1)S(1)} %pad_maximum_fusion.1), channel_id=1, source_target_pairs={{0,16},{4,20},{8,24},{12,28},{16,0},{20,4},{24,8},{28,12},{1,17},{... | collective-permute-start | bytes 1572872 | tf_op jit(solution)/shard_map/ppermute | solution.py:16
  94.9 5.8 %copy-start.3 = (bf16[1024,2048]{1,0:T(8,128)(2,1)S(1)}, bf16[1024,2048]{1,0:T(8,128)(2,1)}, u32[]{:S(2)}) copy-start(bf16[1024,2048]{1,0:T(8,128)(2,1)} %param.13) | copy-start | bytes 12582916
Sparse Core Ops, SparseCore 0:
  103.4 30.9 reduce-scatter.1
